TPU v7x, 32 devices: a whole 2x2x4 slice. The times are simulated.
32 devices in a mesh: head: 4 (over z), blk: 8 (over y, x, core).
Axes of the slice: x: 2, y: 2, z: 4, core: 2. Of those that a mesh axis runs over, the one named last changes fastest.
Arguments:
- tokens: bfloat16 [2, 2048, 1024], P(None, ('head', 'blk')), may hold values from -6 to 6
- positions: int32 [2, 2048], P(None, ('head', 'blk')), may hold values from 0 to 2047
- time_index: int32 [2], replicated, may hold values from 0 to 63
- time_table: float32 [64, 256], replicated, may hold values from -6 to 6
- w_qkv: bfloat16 [1024, 3072], P(('head', 'blk')), may hold values from -0.21875 to 0.21875
- w_out: bfloat16 [1024, 1024], P(('head', 'blk')), may hold values from -3 to 3
- w_up: bfloat16 [1024, 4096], P(('head', 'blk')), may hold values from -0.1875 to 0.1875
- w_down: bfloat16 [4096, 1024], P(('head', 'blk')), may hold values from -0.09375 to 0.09375
- scale_attn: bfloat16 [256, 1024], P(('head', 'blk')), may hold values from -0.19921875 to 0.19921875
- scale_mlp: bfloat16 [256, 1024], P(('head', 'blk')), may hold values from -0.19921875 to 0.19921875
- cotangent: bfloat16 [2, 2048, 1024], P(None, ('head', 'blk')), may hold values from -6 to 6
Outputs:
- output: bfloat16 [2, 2048, 1024], P(None, ('head', 'blk'))
- grad_tokens: float32 [2, 2048, 1024], P(None, ('head', 'blk'))
- grad_w_qkv: float32 [1024, 3072], P(('head', 'blk'))
- grad_w_out: float32 [1024, 1024], P(('head', 'blk'))
- grad_w_up: float32 [1024, 4096], P(('head', 'blk'))
- grad_w_down: float32 [4096, 1024], P(('head', 'blk'))
- grad_scale_attn: float32 [256, 1024], P(('head', 'blk'))
- grad_scale_mlp: float32 [256, 1024], P(('head', 'blk'))
All inputs are finite; a program needn't handle non-finite values.
Results may differ from a plain program's by a relative error of at most 0.017.
Values may be sent and summed in bfloat16 or wider, within the bound.
A program may use at most 256 MiB of HBM per device.

v0:
```python
import math
import jax
import jax.numpy as jnp
from jax import lax
from jax.sharding import PartitionSpec as P

HEADS = 16
HEAD_DIM = 64
NORM_EPSILON = 1e-05
PRECISE = lax.Precision.HIGHEST
START_TOP = -1e30
SCORE_SCALE = 0.125


def shifted(value, axis, steps):
    count = lax.axis_size(axis)
    pairs = [(source, (source + steps) % count) for source in range(count)]
    return lax.ppermute(value, axis, pairs)


def layer_norm(value, scale):
    centered = value - jnp.mean(value, axis=-1, keepdims=True)
    variance = jnp.mean(centered * centered, axis=-1, keepdims=True)
    return centered * lax.rsqrt(variance + NORM_EPSILON) * scale


def rotate(value, cosine_table, sine_table):
    half_dim = value.shape[-1] // 2
    first_half = value[..., :half_dim]
    second_half = value[..., half_dim:]
    return jnp.concatenate(
        [
            first_half * cosine_table - second_half * sine_table,
            second_half * cosine_table + first_half * sine_table,
        ],
        axis=-1,
    )


def rotary_tables(positions, head_dim):
    half_dim = head_dim // 2
    frequency = 10000.0 ** (-jnp.arange(half_dim, dtype=jnp.float32) / half_dim)
    turned = positions.astype(jnp.float32)[:, :, None, None] * frequency
    return (jnp.cos(turned), jnp.sin(turned))


def contract_rows(left, right):
    return lax.dot_general(
        left, right, (((0,), (0,)), ((), ())), preferred_element_type=jnp.float32
    )


def contract_cols(left, right):
    return lax.dot_general(
        left, right, (((1,), (1,)), ((), ())), preferred_element_type=jnp.float32
    )


def attend_step(running, query_block, key_block, value_block):
    row_top, row_sum, accum = running
    scores = (
        jnp.einsum("sqhd,skhd->sqhk", query_block, key_block, preferred_element_type=jnp.float32)
        * SCORE_SCALE
    )
    new_top = jnp.maximum(row_top, jnp.max(scores, axis=-1))
    shrink = jnp.exp(row_top - new_top)
    weights = jnp.exp(scores - new_top[..., None])
    row_sum = row_sum * shrink + jnp.sum(weights, axis=-1)
    accum = accum * shrink[..., None] + jnp.einsum(
        "sqhk,skhd->sqhd",
        weights.astype(jnp.bfloat16),
        value_block,
        preferred_element_type=jnp.float32,
    )
    return (new_top, row_sum, accum)


def back_step(query_block, key_block, value_block, grad_block, log_total, delta):
    scores = (
        jnp.einsum("sqhd,skhd->sqhk", query_block, key_block, preferred_element_type=jnp.float32)
        * SCORE_SCALE
    )
    probs = jnp.exp(scores - log_total[..., None])
    grad_values = jnp.einsum(
        "sqhk,sqhd->skhd",
        probs.astype(jnp.bfloat16),
        grad_block,
        preferred_element_type=jnp.float32,
    )
    grad_probs = jnp.einsum(
        "sqhd,skhd->sqhk", grad_block, value_block, preferred_element_type=jnp.float32
    )
    grad_scores = (probs * (grad_probs - delta[..., None])).astype(jnp.bfloat16)
    grad_query = jnp.einsum(
        "sqhk,skhd->sqhd", grad_scores, key_block, preferred_element_type=jnp.float32
    )
    grad_keys = jnp.einsum(
        "sqhk,sqhd->skhd", grad_scores, query_block, preferred_element_type=jnp.float32
    )
    return (grad_query, grad_keys, grad_values)


def local(
    tokens,
    positions,
    time_index,
    time_table,
    w_qkv,
    w_out,
    w_up,
    w_down,
    scale_attn,
    scale_mlp,
    cotangent,
):
    seq_count, row_count, model_width = tokens.shape
    group_count = lax.axis_size("head")
    local_heads = HEADS // group_count
    feature_width = local_heads * HEAD_DIM
    flat_rows = seq_count * row_count
    gathered = (
        lax.all_gather(w_qkv, ("head", "blk"), axis=0, tiled=True),
        lax.all_gather(w_out, ("head", "blk"), axis=0, tiled=True),
        lax.all_gather(w_up, ("head", "blk"), axis=0, tiled=True),
        lax.all_gather(w_down, ("head", "blk"), axis=0, tiled=True),
        lax.all_gather(scale_attn, ("head", "blk"), axis=0, tiled=True),
        lax.all_gather(scale_mlp, ("head", "blk"), axis=0, tiled=True),
    )
    full_qkv, full_out, full_up, full_down, full_scale_attn, full_scale_mlp = gathered
    step_count = time_table.shape[0]
    picker = (time_index[:, None] == jnp.arange(step_count, dtype=jnp.int32)[None, :]).astype(
        jnp.float32
    )
    time_embed = jnp.dot(picker, time_table, precision=PRECISE)
    scale_one = 1.0 + jnp.dot(time_embed, full_scale_attn.astype(jnp.float32), precision=PRECISE)
    scale_two = 1.0 + jnp.dot(time_embed, full_scale_mlp.astype(jnp.float32), precision=PRECISE)
    token_float = tokens.astype(jnp.float32)
    normed = (
        layer_norm(token_float, scale_one[:, None, :])
        .astype(jnp.bfloat16)
        .reshape(flat_rows, model_width)
    )
    projected = jnp.dot(normed, full_qkv, preferred_element_type=jnp.float32).reshape(
        seq_count, row_count, 3, HEADS, HEAD_DIM
    )
    cosine_table, sine_table = rotary_tables(positions, HEAD_DIM)
    query_tok = rotate(projected[:, :, 0], cosine_table, sine_table)
    keys_tok = rotate(projected[:, :, 1], cosine_table, sine_table)
    packed = (
        jnp.stack([query_tok, keys_tok, projected[:, :, 2]], axis=2)
        .reshape(seq_count, row_count, 3, model_width)
        .astype(jnp.bfloat16)
    )
    regrouped = lax.all_to_all(packed, "head", split_axis=3, concat_axis=1, tiled=True)
    block_len = regrouped.shape[1]
    local_query = regrouped[:, :, 0].reshape(seq_count, block_len, local_heads, HEAD_DIM)
    local_keys = regrouped[:, :, 1]
    local_values = regrouped[:, :, 2]
    start_state = (
        jnp.full((seq_count, block_len, local_heads), START_TOP, jnp.float32),
        jnp.zeros((seq_count, block_len, local_heads), jnp.float32),
        jnp.zeros((seq_count, block_len, local_heads, HEAD_DIM), jnp.float32),
    )
    key_piece = lax.all_gather(local_keys, "blk", axis=1, tiled=True)
    value_piece = lax.all_gather(local_values, "blk", axis=1, tiled=True)
    piece_len = key_piece.shape[1]
    step_len = math.gcd(piece_len, block_len)

    def one_block(index, state):
        key_block = lax.dynamic_slice_in_dim(key_piece, index * step_len, step_len, 1).reshape(
            seq_count, step_len, local_heads, HEAD_DIM
        )
        value_block = lax.dynamic_slice_in_dim(value_piece, index * step_len, step_len, 1).reshape(
            seq_count, step_len, local_heads, HEAD_DIM
        )
        return attend_step(state, local_query, key_block, value_block)

    row_top, row_sum, accum = lax.fori_loop(0, piece_len // step_len, one_block, start_state)
    mixed = accum / row_sum[..., None]
    log_total = row_top + jnp.log(row_sum)
    attended_heads = mixed.astype(jnp.bfloat16).reshape(seq_count, block_len, feature_width)
    attended = lax.all_to_all(
        attended_heads, "head", split_axis=1, concat_axis=2, tiled=True
    ).reshape(flat_rows, model_width)
    branch = jnp.dot(attended, full_out, preferred_element_type=jnp.float32)
    middle = token_float + branch.reshape(seq_count, row_count, model_width)
    normed_two = (
        layer_norm(middle, scale_two[:, None, :])
        .astype(jnp.bfloat16)
        .reshape(flat_rows, model_width)
    )
    hidden = jnp.dot(normed_two, full_up, preferred_element_type=jnp.float32)
    active = jax.nn.gelu(hidden, approximate=False).astype(jnp.bfloat16)
    result = middle.reshape(flat_rows, model_width) + jnp.dot(
        active, full_down, preferred_element_type=jnp.float32
    )
    output = result.astype(jnp.bfloat16).reshape(seq_count, row_count, model_width)
    back_qkv, back_out, back_up, back_down = (
        lax.all_gather(w_qkv, ("head", "blk"), axis=0, tiled=True),
        lax.all_gather(w_out, ("head", "blk"), axis=0, tiled=True),
        lax.all_gather(w_up, ("head", "blk"), axis=0, tiled=True),
        lax.all_gather(w_down, ("head", "blk"), axis=0, tiled=True),
    )
    grad_out = cotangent.reshape(flat_rows, model_width)
    grad_active = contract_cols(grad_out, back_down)
    grad_w_down = contract_rows(active, grad_out)
    gelu_value, gelu_pull = jax.vjp(lambda entry: jax.nn.gelu(entry, approximate=False), hidden)
    grad_hidden = gelu_pull(grad_active)[0].astype(jnp.bfloat16)
    grad_w_up = contract_rows(normed_two, grad_hidden)
    grad_normed_two = contract_cols(grad_hidden, back_up).reshape(seq_count, row_count, model_width)
    norm_value, norm_pull = jax.vjp(layer_norm, middle, scale_two[:, None, :])
    grad_middle_norm, grad_scale_two = norm_pull(grad_normed_two)
    grad_middle = cotangent.astype(jnp.float32) + grad_middle_norm
    grad_scale_mlp = jnp.dot(time_embed.T, grad_scale_two[:, 0, :], precision=PRECISE)
    grad_branch = grad_middle.reshape(flat_rows, model_width).astype(jnp.bfloat16)
    grad_w_out = contract_rows(attended, grad_branch)
    grad_attended = (
        contract_cols(grad_branch, back_out)
        .astype(jnp.bfloat16)
        .reshape(seq_count, row_count, model_width)
    )
    grad_heads = lax.all_to_all(
        grad_attended, "head", split_axis=2, concat_axis=1, tiled=True
    ).reshape(seq_count, block_len, local_heads, HEAD_DIM)
    delta = jnp.sum(grad_heads.astype(jnp.float32) * mixed, axis=-1)

    def turn(index, state):
        key_now, value_now, grad_keys_now, grad_values_now, grad_query_sum = state
        grad_query, grad_keys, grad_values = back_step(
            local_query,
            key_now.reshape(seq_count, block_len, local_heads, HEAD_DIM),
            value_now.reshape(seq_count, block_len, local_heads, HEAD_DIM),
            grad_heads,
            log_total,
            delta,
        )
        moved_keys, moved_values = shifted((key_now, value_now), "blk", 1)
        moved_grad_keys, moved_grad_values = (
            shifted(
                (grad_keys_now + grad_keys.reshape(seq_count, block_len, feature_width)).astype(
                    jnp.bfloat16
                ),
                "blk",
                1,
            ).astype(jnp.float32),
            shifted(
                (grad_values_now + grad_values.reshape(seq_count, block_len, feature_width)).astype(
                    jnp.bfloat16
                ),
                "blk",
                1,
            ).astype(jnp.float32),
        )
        return (
            moved_keys,
            moved_values,
            moved_grad_keys,
            moved_grad_values,
            grad_query_sum + grad_query,
        )

    zero_kv = jnp.zeros((seq_count, block_len, feature_width), jnp.float32)
    begin = (
        local_keys,
        local_values,
        zero_kv,
        zero_kv,
        jnp.zeros((seq_count, block_len, local_heads, HEAD_DIM), jnp.float32),
    )
    final_state = lax.fori_loop(0, lax.axis_size("blk"), turn, begin)
    grad_keys_own = final_state[2]
    grad_values_own = final_state[3]
    grad_query_all = final_state[4]
    stacked = jnp.stack(
        [
            grad_query_all.reshape(seq_count, block_len, feature_width) * SCORE_SCALE,
            grad_keys_own * SCORE_SCALE,
            grad_values_own,
        ],
        axis=2,
    ).astype(jnp.bfloat16)
    returned = lax.all_to_all(stacked, "head", split_axis=1, concat_axis=3, tiled=True)
    grad_query_tok = (
        returned[:, :, 0].astype(jnp.float32).reshape(seq_count, row_count, HEADS, HEAD_DIM)
    )
    grad_keys_tok = (
        returned[:, :, 1].astype(jnp.float32).reshape(seq_count, row_count, HEADS, HEAD_DIM)
    )
    grad_values_tok = (
        returned[:, :, 2].astype(jnp.float32).reshape(seq_count, row_count, HEADS, HEAD_DIM)
    )
    grad_projected = (
        jnp.stack(
            [
                rotate(grad_query_tok, cosine_table, -sine_table),
                rotate(grad_keys_tok, cosine_table, -sine_table),
                grad_values_tok,
            ],
            axis=2,
        )
        .reshape(flat_rows, 3 * model_width)
        .astype(jnp.bfloat16)
    )
    grad_w_qkv = contract_rows(normed, grad_projected)
    grad_normed = contract_cols(grad_projected, back_qkv).reshape(seq_count, row_count, model_width)
    first_value, first_pull = jax.vjp(layer_norm, token_float, scale_one[:, None, :])
    grad_token_norm, grad_scale_one = first_pull(grad_normed)
    grad_tokens = grad_middle + grad_token_norm
    grad_scale_attn = jnp.dot(time_embed.T, grad_scale_one[:, 0, :], precision=PRECISE)
    shards = (
        lax.psum_scatter(grad_w_qkv, ("head", "blk"), scatter_dimension=0, tiled=True),
        lax.psum_scatter(grad_w_out, ("head", "blk"), scatter_dimension=0, tiled=True),
        lax.psum_scatter(grad_w_up, ("head", "blk"), scatter_dimension=0, tiled=True),
        lax.psum_scatter(grad_w_down, ("head", "blk"), scatter_dimension=0, tiled=True),
        lax.psum_scatter(grad_scale_attn, ("head", "blk"), scatter_dimension=0, tiled=True),
        lax.psum_scatter(grad_scale_mlp, ("head", "blk"), scatter_dimension=0, tiled=True),
    )
    return (output, grad_tokens, shards[0], shards[1], shards[2], shards[3], shards[4], shards[5])


def solution(mesh):
    placed = (
        P(None, ("head", "blk"), None),
        P(None, ("head", "blk")),
        P(),
        P(),
        P(("head", "blk"), None),
        P(("head", "blk"), None),
        P(("head", "blk"), None),
        P(("head", "blk"), None),
        P(("head", "blk"), None),
        P(("head", "blk"), None),
        P(None, ("head", "blk"), None),
    )
    return jax.shard_map(
        local,
        mesh=mesh,
        in_specs=placed,
        out_specs=(
            P(None, ("head", "blk"), None),
            P(None, ("head", "blk"), None),
            P(("head", "blk"), None),
            P(("head", "blk"), None),
            P(("head", "blk"), None),
            P(("head", "blk"), None),
            P(("head", "blk"), None),
            P(("head", "blk"), None),
        ),
        check_vma=False,
    )
```

profile of v0, /device:TPU:14, one launch (start us, length us, event | category | flops | bytes accessed | tf_op | source)
XLA Modules:
  0.0 1571.5 jit_solution(9554093618369805315)
XLA Ops:
  12.5 30.9 %all_gather.28 = bf16[256,1024]{1,0:T(8,128)(2,1)S(1)} all-gather(bf16[8,1024]{1,0:T(8,128)(2,1)} %param.23), channel_id=1, replica_groups=mesh['head'=4,'blk'=8] {'head','blk'}, dimensions={0}, use_global_device_ids=true | all-gather | bytes 540672 | tf_op jit(solution)/shard_map/all_gather | solution.py:126
  44.0 37.4 %all-gather.9.cloned.1.call-done = bf16[1024,3072]{1,0:T(8,128)(2,1)} async-done(((bf16[32,3072]{1,0:T(8,128)(2,1)}), bf16[1024,3072]{1,0:T(8,128)(2,1)}) %all-gather.9.cloned.1.call-update) | async-done | bytes 6291472 | tf_op jit(solution)/shard_map/all_gather | solution.py:122
  81.5 8.6 copy.148
  90.1 4.5 fusion.47
  97.1 2.9 fusion.60
  101.4 22.1 %all_to_all.66 = bf16[4,2,49152]{2,1,0:T(2,128)(2,1)S(1)} all-to-all(bf16[4,2,49152]{2,1,0:T(2,128)(2,1)S(1)} %reshape.240), channel_id=1, replica_groups=mesh['head'=4,'blk'=8] {'head'}, dimensions={0} | all-to-all | bytes 1572864 | tf_op jit(solution)/shard_map/all_to_all | solution.py:154
  124.7 2.3 copy.182
  130.8 24.8 %all-gather.17.cloned.1.call-done = bf16[2,2048,1,256]{3,1,2,0:T(8,128)(2,1)} async-done(((bf16[2,256,1,256]{3,1,2,0:T(8,128)(2,1)}), bf16[2,2048,1,256]{3,1,2,0:T(8,128)(2,1)}) %all-gather.17.cloned.1.call-update) | async-done | bytes 2097168 | tf_op jit(solution)/shard_map/all_gather | solution.py:164
  155.6 30.4 %all-gather.19.cloned.1.call-done = bf16[2,2048,1,256]{3,1,2,0:T(8,128)(2,1)} async-done(((bf16[2,256,1,256]{3,1,2,0:T(8,128)(2,1)}), bf16[2,2048,1,256]{3,1,2,0:T(8,128)(2,1)}) %all-gather.19.cloned.1.call-update) | async-done | bytes 2097168 | tf_op jit(solution)/shard_map/all_gather | solution.py:165
  186.1 22.7 %while.37 = (s32[]{:T(128)}, f32[2,256,4]{1,2,0:T(4,128)S(1)}, f32[2,256,4]{1,2,0:T(4,128)S(1)}, f32[2,256,4,64]{1,3,2,0:T(8,128)S(1)}, bf16[2,2048,256]{2,1,0:T...) while((s32[]{:T(128)}, f32[2,256,4]{1,2,0:T(4,128)S(1)}, ...), condition=%wide.region_5.0_spmd.clone, body=%wide.region_2.0_spmd.clone.sunk | while | flops 138815488 | bytes 10354867 | solution.py:178
  209.7 5.1 all-to-all-start.1
  214.8 35.6 %all_gather.33 = bf16[256,1024]{1,0:T(8,128)(2,1)S(1)} all-gather(bf16[8,1024]{1,0:T(8,128)(2,1)S(1)} %copy-done.38), channel_id=1, replica_groups=mesh['head'=4,'blk'=8] {'head','blk'}, dimensions={0}, use_global_device_ids=true | all-gather | bytes 540672 | tf_op jit(solution)/shard_map/all_gather | solution.py:127
  251.5 2.1 fusion.59
  254.7 71.0 %all-gather.13.cloned.1.call-done = bf16[1024,4096]{1,0:T(8,128)(2,1)} async-done(((bf16[32,4096]{1,0:T(8,128)(2,1)}), bf16[1024,4096]{1,0:T(8,128)(2,1)}) %all-gather.13.cloned.1.call-update) | async-done | bytes 8388624 | tf_op jit(solution)/shard_map/all_gather | solution.py:124
  325.7 4.7 fusion.63
  330.5 74.0 %all-gather.15.cloned.1.call-done = bf16[4096,1024]{1,0:T(8,128)(2,1)} async-done(((bf16[128,1024]{1,0:T(8,128)(2,1)}), bf16[4096,1024]{1,0:T(8,128)(2,1)}) %all-gather.15.cloned.1.call-update) | async-done | bytes 8388624 | tf_op jit(solution)/shard_map/all_gather | solution.py:125
  404.5 10.4 add_convert_fusion
  414.9 2.9 fusion.64
  419.9 2.5 convolution_convert_fusion
  423.9 4.0 all-to-all-start.2
  429.7 5.9 all-to-all-done.2
  438.5 169.7 %while.38 = (s32[]{:T(128)}, bf16[2,256,256]{1,2,0:T(8,128)(2,1)}, bf16[2,256,256]{1,2,0:T(8,128)(2,1)}, f32[2,256,256]{1,2,0:T(8,128)}, f32[2,256,256]{1,2,0:T(...) while((s32[]{:T(128)}, bf16[2,256,256]{1,2,0:T(8,128)(2,1)}, ...), condition=%wide.region_12.0_spmd.clone, body=%wide.region_11.0_spmd.clone.sunk | while | flops 341049344 | bytes 24928572 | solution.py:270
  452.8 2.1 fusion.160
  462.7 2.4 collective-permute-start.1
  473.8 2.3 fusion.160
  494.8 2.3 fusion.160
  515.8 2.3 fusion.160
  537.7 2.3 fusion.160
  547.6 2.4 collective-permute-start.1
  558.7 2.3 fusion.160
  579.7 2.3 fusion.160
  600.7 2.3 fusion.160
  613.4 5.4 all-to-all-start.3
  618.8 2.0 fusion.70
  620.9 13.6 all-to-all-done.3
  640.6 5.1 fusion.44
  648.4 2.7 fusion.66
  652.6 6.3 fusion.65
  660.2 8.1 fusion.67
  668.4 2.5 multiply_convert_fusion
  670.9 8.1 fusion.68
  680.1 5.4 fusion.34
  686.8 39.8 %reduce-scatter.17.cloned.1.call-done = f32[8,1024]{1,0:T(8,128)} async-done(((f32[256,1024]{1,0:T(8,128)}), f32[8,1024]{1,0:T(8,128)}) %reduce-scatter.17.cloned.1.call-update) | async-done | bytes 32784 | tf_op jit(solution)/shard_map/reduce_scatter | solution.py:316
  726.6 133.1 %reduce-scatter.15.cloned.1.call-done = f32[8,1024]{1,0:T(8,128)} async-done(((f32[256,1024]{1,0:T(8,128)}), f32[8,1024]{1,0:T(8,128)}) %reduce-scatter.15.cloned.1.call-update) | async-done | bytes 32784 | tf_op jit(solution)/shard_map/reduce_scatter | solution.py:315
  859.7 139.6 %reduce-scatter.9.cloned.1.call-done = f32[32,1024]{1,0:T(8,128)} async-done(((f32[1024,1024]{1,0:T(8,128)}), f32[32,1024]{1,0:T(8,128)}) %reduce-scatter.9.cloned.1.call-update) | async-done | bytes 131088 | tf_op jit(solution)/shard_map/reduce_scatter | solution.py:312
  999.3 190.4 %reduce-scatter.7.cloned.1.call-done = f32[32,3072]{1,0:T(8,128)} async-done(((f32[1024,3072]{1,0:T(8,128)}), f32[32,3072]{1,0:T(8,128)}) %reduce-scatter.7.cloned.1.call-update) | async-done | bytes 393232 | tf_op jit(solution)/shard_map/reduce_scatter | solution.py:311
  1189.6 187.4 %reduce-scatter.11.cloned.1.call-done = f32[32,4096]{1,0:T(8,128)} async-done(((f32[1024,4096]{1,0:T(8,128)}), f32[32,4096]{1,0:T(8,128)}) %reduce-scatter.11.cloned.1.call-update) | async-done | bytes 524304 | tf_op jit(solution)/shard_map/reduce_scatter | solution.py:313
  1377.1 187.3 %reduce-scatter.13.cloned.1.call-done = f32[128,1024]{1,0:T(8,128)} async-done(((f32[4096,1024]{1,0:T(8,128)}), f32[128,1024]{1,0:T(8,128)}) %reduce-scatter.13.cloned.1.call-update) | async-done | bytes 524304 | tf_op jit(solution)/shard_map/reduce_scatter | solution.py:314
  (417 shorter events, 213.3 us)
Async XLA Ops:
  7.2 74.3 %all-gather.9.cloned.1.call-start = ((), (), s32[]{:S(2)}) async-start(), calls=%async_computation.10 | async-start | bytes 6488064 | tf_op jit(solution)/shard_map/all_gather | solution.py:122
  7.9 147.7 %all-gather.17.cloned.1.call-start = ((), (), s32[]{:S(2)}) async-start(), calls=%async_computation.20 | async-start | bytes 2359296 | tf_op jit(solution)/shard_map/all_gather | solution.py:164
  128.2 57.9 %all-gather.19.cloned.1.call-start = ((), (), s32[]{:S(2)}) async-start(), calls=%async_computation.21 | async-start | bytes 2359296 | tf_op jit(solution)/shard_map/all_gather | solution.py:165
  128.9 121.9 %all-gather.11.cloned.1.call-start = ((), (), s32[]{:S(2)}) async-start(), calls=%async_computation.11 | async-start | bytes 2162688 | tf_op jit(solution)/shard_map/all_gather | solution.py:123
  129.5 196.2 %all-gather.13.cloned.1.call-start = ((), (), s32[]{:S(2)}) async-start(), calls=%async_computation.12 | async-start | bytes 8650752 | tf_op jit(solution)/shard_map/all_gather | solution.py:124
  130.1 274.4 %all-gather.15.cloned.1.call-start = ((), (), s32[]{:S(2)}) async-start(), calls=%async_computation.13 | async-start | bytes 8650752 | tf_op jit(solution)/shard_map/all_gather | solution.py:125
  209.7 41.0 %all-to-all-start.1 = ((bf16[2,256,256]{2,0,1:T(2,128)(2,1)}), bf16[2,256,256]{2,0,1:T(2,128)(2,1)S(1)}, u32[]{:S(2)}, u32[]{:S(2)}) async-start(bf16[2,256,256]{2,0,1:T(2,128)(2,1)} %copy.158), calls=%async_computation.1 | async-start | bytes 524288 | tf_op jit(solution)/shard_map/all_to_all | solution.py:182
  423.9 11.7 all-to-all-start.2
  440.1 19.2 %collective-permute-start = (bf16[2,256,256]{1,2,0:T(8,128)(2,1)}, bf16[2,256,256]{1,2,0:T(8,128)(2,1)}, u32[]{:S(2)}, u32[]{:S(2)}) collective-permute-start(bf16[2,256,256]{1,2,0:T(8,128)(2,1)} %copy.218), channel_id=1, source_target_pairs={{0,1},{1,2},{2,3},{3,4},{4,5},{5,6},{6,7},{7,0},{8,9},{9,10},{10,1... | collective-permute-start | bytes 786440 | tf_op jit(solution)/shard_map/while/body/eval_jaxpr/ppermute | solution.py:18
  441.8 17.5 %collective-permute-start.1 = (bf16[2,256,256]{1,2,0:T(8,128)(2,1)}, bf16[2,256,256]{1,2,0:T(8,128)(2,1)}, u32[]{:S(2)}, u32[]{:S(2)}) collective-permute-start(bf16[2,256,256]{1,2,0:T(8,128)(2,1)} %copy.219), channel_id=1, source_target_pairs={{0,1},{1,2},{2,3},{3,4},{4,5},{5,6},{6,7},{7,0},{8,9},{9,10},{10,1... | collective-permute-start | bytes 786440 | tf_op jit(solution)/shard_map/while/body/eval_jaxpr/ppermute | solution.py:18
  449.7 6.1 collective-permute-start.2
  451.2 7.3 collective-permute-start.3
  461.0 20.2 %collective-permute-start = (bf16[2,256,256]{1,2,0:T(8,128)(2,1)}, bf16[2,256,256]{1,2,0:T(8,128)(2,1)}, u32[]{:S(2)}, u32[]{:S(2)}) collective-permute-start(bf16[2,256,256]{1,2,0:T(8,128)(2,1)} %copy.218), channel_id=1, source_target_pairs={{0,1},{1,2},{2,3},{3,4},{4,5},{5,6},{6,7},{7,0},{8,9},{9,10},{10,1... | collective-permute-start | bytes 786440 | tf_op jit(solution)/shard_map/while/body/eval_jaxpr/ppermute | solution.py:18
  462.7 18.5 %collective-permute-start.1 = (bf16[2,256,256]{1,2,0:T(8,128)(2,1)}, bf16[2,256,256]{1,2,0:T(8,128)(2,1)}, u32[]{:S(2)}, u32[]{:S(2)}) collective-permute-start(bf16[2,256,256]{1,2,0:T(8,128)(2,1)} %copy.219), channel_id=1, source_target_pairs={{0,1},{1,2},{2,3},{3,4},{4,5},{5,6},{6,7},{7,0},{8,9},{9,10},{10,1... | collective-permute-start | bytes 786440 | tf_op jit(solution)/shard_map/while/body/eval_jaxpr/ppermute | solution.py:18
  471.5 6.1 collective-permute-start.2
  473.1 7.3 collective-permute-start.3
  482.9 19.4 %collective-permute-start = (bf16[2,256,256]{1,2,0:T(8,128)(2,1)}, bf16[2,256,256]{1,2,0:T(8,128)(2,1)}, u32[]{:S(2)}, u32[]{:S(2)}) collective-permute-start(bf16[2,256,256]{1,2,0:T(8,128)(2,1)} %copy.218), channel_id=1, source_target_pairs={{0,1},{1,2},{2,3},{3,4},{4,5},{5,6},{6,7},{7,0},{8,9},{9,10},{10,1... | collective-permute-start | bytes 786440 | tf_op jit(solution)/shard_map/while/body/eval_jaxpr/ppermute | solution.py:18
  484.5 17.7 %collective-permute-start.1 = (bf16[2,256,256]{1,2,0:T(8,128)(2,1)}, bf16[2,256,256]{1,2,0:T(8,128)(2,1)}, u32[]{:S(2)}, u32[]{:S(2)}) collective-permute-start(bf16[2,256,256]{1,2,0:T(8,128)(2,1)} %copy.219), channel_id=1, source_target_pairs={{0,1},{1,2},{2,3},{3,4},{4,5},{5,6},{6,7},{7,0},{8,9},{9,10},{10,1... | collective-permute-start | bytes 786440 | tf_op jit(solution)/shard_map/while/body/eval_jaxpr/ppermute | solution.py:18
  492.6 6.1 collective-permute-start.2
  494.1 7.3 collective-permute-start.3
  503.9 19.3 %collective-permute-start = (bf16[2,256,256]{1,2,0:T(8,128)(2,1)}, bf16[2,256,256]{1,2,0:T(8,128)(2,1)}, u32[]{:S(2)}, u32[]{:S(2)}) collective-permute-start(bf16[2,256,256]{1,2,0:T(8,128)(2,1)} %copy.218), channel_id=1, source_target_pairs={{0,1},{1,2},{2,3},{3,4},{4,5},{5,6},{6,7},{7,0},{8,9},{9,10},{10,1... | collective-permute-start | bytes 786440 | tf_op jit(solution)/shard_map/while/body/eval_jaxpr/ppermute | solution.py:18
  505.6 17.7 %collective-permute-start.1 = (bf16[2,256,256]{1,2,0:T(8,128)(2,1)}, bf16[2,256,256]{1,2,0:T(8,128)(2,1)}, u32[]{:S(2)}, u32[]{:S(2)}) collective-permute-start(bf16[2,256,256]{1,2,0:T(8,128)(2,1)} %copy.219), channel_id=1, source_target_pairs={{0,1},{1,2},{2,3},{3,4},{4,5},{5,6},{6,7},{7,0},{8,9},{9,10},{10,1... | collective-permute-start | bytes 786440 | tf_op jit(solution)/shard_map/while/body/eval_jaxpr/ppermute | solution.py:18
  513.6 6.1 collective-permute-start.2
  515.1 7.3 collective-permute-start.3
  524.9 19.3 %collective-permute-start = (bf16[2,256,256]{1,2,0:T(8,128)(2,1)}, bf16[2,256,256]{1,2,0:T(8,128)(2,1)}, u32[]{:S(2)}, u32[]{:S(2)}) collective-permute-start(bf16[2,256,256]{1,2,0:T(8,128)(2,1)} %copy.218), channel_id=1, source_target_pairs={{0,1},{1,2},{2,3},{3,4},{4,5},{5,6},{6,7},{7,0},{8,9},{9,10},{10,1... | collective-permute-start | bytes 786440 | tf_op jit(solution)/shard_map/while/body/eval_jaxpr/ppermute | solution.py:18
  526.6 17.6 %collective-permute-start.1 = (bf16[2,256,256]{1,2,0:T(8,128)(2,1)}, bf16[2,256,256]{1,2,0:T(8,128)(2,1)}, u32[]{:S(2)}, u32[]{:S(2)}) collective-permute-start(bf16[2,256,256]{1,2,0:T(8,128)(2,1)} %copy.219), channel_id=1, source_target_pairs={{0,1},{1,2},{2,3},{3,4},{4,5},{5,6},{6,7},{7,0},{8,9},{9,10},{10,1... | collective-permute-start | bytes 786440 | tf_op jit(solution)/shard_map/while/body/eval_jaxpr/ppermute | solution.py:18
  534.6 6.1 collective-permute-start.2
  536.1 7.3 collective-permute-start.3
  545.9 20.2 %collective-permute-start = (bf16[2,256,256]{1,2,0:T(8,128)(2,1)}, bf16[2,256,256]{1,2,0:T(8,128)(2,1)}, u32[]{:S(2)}, u32[]{:S(2)}) collective-permute-start(bf16[2,256,256]{1,2,0:T(8,128)(2,1)} %copy.218), channel_id=1, source_target_pairs={{0,1},{1,2},{2,3},{3,4},{4,5},{5,6},{6,7},{7,0},{8,9},{9,10},{10,1... | collective-permute-start | bytes 786440 | tf_op jit(solution)/shard_map/while/body/eval_jaxpr/ppermute | solution.py:18
  547.6 18.5 %collective-permute-start.1 = (bf16[2,256,256]{1,2,0:T(8,128)(2,1)}, bf16[2,256,256]{1,2,0:T(8,128)(2,1)}, u32[]{:S(2)}, u32[]{:S(2)}) collective-permute-start(bf16[2,256,256]{1,2,0:T(8,128)(2,1)} %copy.219), channel_id=1, source_target_pairs={{0,1},{1,2},{2,3},{3,4},{4,5},{5,6},{6,7},{7,0},{8,9},{9,10},{10,1... | collective-permute-start | bytes 786440 | tf_op jit(solution)/shard_map/while/body/eval_jaxpr/ppermute | solution.py:18
  556.4 6.1 collective-permute-start.2
  558.0 7.3 collective-permute-start.3
  567.8 19.4 %collective-permute-start = (bf16[2,256,256]{1,2,0:T(8,128)(2,1)}, bf16[2,256,256]{1,2,0:T(8,128)(2,1)}, u32[]{:S(2)}, u32[]{:S(2)}) collective-permute-start(bf16[2,256,256]{1,2,0:T(8,128)(2,1)} %copy.218), channel_id=1, source_target_pairs={{0,1},{1,2},{2,3},{3,4},{4,5},{5,6},{6,7},{7,0},{8,9},{9,10},{10,1... | collective-permute-start | bytes 786440 | tf_op jit(solution)/shard_map/while/body/eval_jaxpr/ppermute | solution.py:18
  569.4 17.7 %collective-permute-start.1 = (bf16[2,256,256]{1,2,0:T(8,128)(2,1)}, bf16[2,256,256]{1,2,0:T(8,128)(2,1)}, u32[]{:S(2)}, u32[]{:S(2)}) collective-permute-start(bf16[2,256,256]{1,2,0:T(8,128)(2,1)} %copy.219), channel_id=1, source_target_pairs={{0,1},{1,2},{2,3},{3,4},{4,5},{5,6},{6,7},{7,0},{8,9},{9,10},{10,1... | collective-permute-start | bytes 786440 | tf_op jit(solution)/shard_map/while/body/eval_jaxpr/ppermute | solution.py:18
  577.5 6.1 collective-permute-start.2
  579.0 7.3 collective-permute-start.3
  588.8 19.3 %collective-permute-start = (bf16[2,256,256]{1,2,0:T(8,128)(2,1)}, bf16[2,256,256]{1,2,0:T(8,128)(2,1)}, u32[]{:S(2)}, u32[]{:S(2)}) collective-permute-start(bf16[2,256,256]{1,2,0:T(8,128)(2,1)} %copy.218), channel_id=1, source_target_pairs={{0,1},{1,2},{2,3},{3,4},{4,5},{5,6},{6,7},{7,0},{8,9},{9,10},{10,1... | collective-permute-start | bytes 786440 | tf_op jit(solution)/shard_map/while/body/eval_jaxpr/ppermute | solution.py:18
  590.5 17.7 %collective-permute-start.1 = (bf16[2,256,256]{1,2,0:T(8,128)(2,1)}, bf16[2,256,256]{1,2,0:T(8,128)(2,1)}, u32[]{:S(2)}, u32[]{:S(2)}) collective-permute-start(bf16[2,256,256]{1,2,0:T(8,128)(2,1)} %copy.219), channel_id=1, source_target_pairs={{0,1},{1,2},{2,3},{3,4},{4,5},{5,6},{6,7},{7,0},{8,9},{9,10},{10,1... | collective-permute-start | bytes 786440 | tf_op jit(solution)/shard_map/while/body/eval_jaxpr/ppermute | solution.py:18
  598.5 6.1 collective-permute-start.2
  600.0 7.3 collective-permute-start.3
  613.4 21.2 %all-to-all-start.3 = ((bf16[2,256,3,256]{3,0,2,1:T(2,128)(2,1)}), bf16[2,256,3,256]{3,0,2,1:T(2,128)(2,1)S(1)}, u32[]{:S(2)}, u32[]{:S(2)}) async-start(bf16[2,256,3,256]{3,0,2,1:T(2,128)(2,1)} %copy.168), calls=%async_computation.3 | async-start | bytes 1572864 | tf_op jit(solution)/shard_map/all_to_all | solution.py:282
  618.8 107.8 %reduce-scatter.17.cloned.1.call-start = ((), (), s32[]{:S(2)}) async-start(), calls=%async_computation.19 | async-start | bytes 1081344 | tf_op jit(solution)/shard_map/reduce_scatter | solution.py:316
  620.9 238.8 %reduce-scatter.15.cloned.1.call-start = ((), (), s32[]{:S(2)}) async-start(), calls=%async_computation.18 | async-start | bytes 1081344 | tf_op jit(solution)/shard_map/reduce_scatter | solution.py:315
  648.1 351.2 %reduce-scatter.9.cloned.1.call-start = ((), (), s32[]{:S(2)}) async-start(), calls=%async_computation.15 | async-start | bytes 4325376 | tf_op jit(solution)/shard_map/reduce_scatter | solution.py:312
  651.2 538.5 %reduce-scatter.7.cloned.1.call-start = ((), (), s32[]{:S(2)}) async-start(), calls=%async_computation.14 | async-start | bytes 12976128 | tf_op jit(solution)/shard_map/reduce_scatter | solution.py:311
  658.9 718.1 %reduce-scatter.11.cloned.1.call-start = ((), (), s32[]{:S(2)}) async-start(), calls=%async_computation.16 | async-start | bytes 17301504 | tf_op jit(solution)/shard_map/reduce_scatter | solution.py:313
  668.3 896.1 %reduce-scatter.13.cloned.1.call-start = ((), (), s32[]{:S(2)}) async-start(), calls=%async_computation.17 | async-start | bytes 17301504 | tf_op jit(solution)/shard_map/reduce_scatter | solution.py:314
  680.1 884.3 %copy-start.1 = (f32[64,256]{1,0:T(8,128)S(1)}, f32[64,256]{1,0:T(8,128)}, u32[]{:S(2)}) copy-start(f32[64,256]{1,0:T(8,128)} %param.18) | copy-start | bytes 196612
  (49 other events, 1095.7 us)
Sparse Core Ops, SparseCore 0:
  10.9 70.5 all-gather.8
  128.3 27.2 all-gather.16
  158.1 27.8 all-gather.18
  188.8 56.9 all-gather.10
  248.4 77.2 all-gather.12
  328.4 76.0 all-gather.14
  622.5 104.0 reduce-scatter.16
  729.5 130.1 reduce-scatter.14
  862.5 136.6 reduce-scatter.8
  1005.7 183.8 reduce-scatter.6
  1192.6 184.4 reduce-scatter.10
  1379.9 184.4 reduce-scatter.12
where the time goes:
time: 1580 us; the launch traced here: 1570 us
  waiting for transfers between devices  1160 us (73%)
  matrix products  141 us (9%)
  blocking collectives  88.7 us (6%)
  local copies, waits for them, and re-layouts  72.9 us (5%)
  other arithmetic  58.9 us (4%)
  starting transfers between devices  37.3 us (2%)
    reduce_scatter x1, waiting for transfers between devices, local(): lax.psum_scatter(grad_w_qkv, ('head', 'blk'), scatter_dimension=0, tiled=...  190 us
    reduce_scatter x1, waiting for transfers between devices, local(): lax.psum_scatter(grad_w_up, ('head', 'blk'), scatter_dimension=0, tiled=T...  187 us
    reduce_scatter x1, waiting for transfers between devices, local(): lax.psum_scatter(grad_w_down, ('head', 'blk'), scatter_dimension=0, tiled...  187 us
    reduce_scatter x1, waiting for transfers between devices, local(): lax.psum_scatter(grad_w_out, ('head', 'blk'), scatter_dimension=0, tiled=...  140 us
    reduce_scatter x1, waiting for transfers between devices, local(): lax.psum_scatter(grad_scale_attn, ('head', 'blk'), scatter_dimension=0, t...  133 us
    all_gather x1, waiting for transfers between devices, local(): lax.all_gather(w_down, ('head', 'blk'), axis=0, tiled=True)  74 us
    all_gather x1, waiting for transfers between devices, local(): lax.all_gather(w_up, ('head', 'blk'), axis=0, tiled=True)  71 us
    reduce_scatter x1, waiting for transfers between devices, local(): lax.psum_scatter(grad_scale_mlp, ('head', 'blk'), scatter_dimension=0, ti...  39.8 us
  transfers between devices with their start and end apart: 47, of which 29 were waited for; matrix products, arithmetic and copies ran while one was open for 13% of the time, Pallas kernels for 0%

commit v1 on v0

--- a/solution.py
+++ b/solution.py
@@ -10,6 +10,26 @@
 PRECISE = lax.Precision.HIGHEST
 START_TOP = -1e30
 SCORE_SCALE = 0.125
+
+
+def supply_spot(m, in_dim):
+    v_next = list(m.shape[1:])
+    v_next[in_dim] *= m.shape[0]
+    return jnp.moveaxis(m, 0, in_dim).reshape(v_next)
+
+
+def form_the_screen(panel, axis_tag):
+    ndev = lax.axis_size(axis_tag)
+    w1 = panel[None]
+    for k0 in range(ndev.bit_length() - 1):
+        wide_out = 1 << k0
+        piece_out = lax.ppermute(
+            w1, axis_tag, list(map(lambda no: (no, no ^ wide_out), range(ndev)))
+        )
+        x_new = jnp.stack([w1, piece_out])
+        oldest = lax.axis_index(axis_tag) >> k0 & 1
+        w1 = jnp.where(oldest == 0, x_new, x_new[::-1]).reshape(-1, *panel.shape)
+    return w1
 
 
 def shifted(value, axis, steps):
@@ -118,8 +138,13 @@
     local_heads = HEADS // group_count
     feature_width = local_heads * HEAD_DIM
     flat_rows = seq_count * row_count
+
+    def _save_samples(u_in, payload, which_dim):
+        fresh = form_the_screen(payload, u_in)
+        return supply_spot(fresh, which_dim)
+
     gathered = (
-        lax.all_gather(w_qkv, ("head", "blk"), axis=0, tiled=True),
+        _save_samples(("head", "blk"), w_qkv, 0),
         lax.all_gather(w_out, ("head", "blk"), axis=0, tiled=True),
         lax.all_gather(w_up, ("head", "blk"), axis=0, tiled=True),
         lax.all_gather(w_down, ("head", "blk"), axis=0, tiled=True),

time: 1580 us -> 1760 us (1.11)
  blocking collectives: 88.7 us -> 216 us
  waiting for transfers between devices: 1160 us -> 1190 us
    all_gather x1, blocking collectives: 30.9 us -> 158 us  [local(): lax.all_gather(scale_attn, ('head', 'blk'), axis=0, tiled=True)]
    ppermute x0 -> x5, waiting for transfers between devices: none -> 64.7 us  [form_the_screen(): lax.ppermute(w1, axis_tag, list(map(lambda no: (no, no ^ wide_out), range...]
    all_gather x1, waiting for transfers between devices: 37.4 us -> 0.02 us  [local(): lax.all_gather(w_qkv, ('head', 'blk'), axis=0, tiled=True)]
  transfers between devices with their start and end apart: 47 -> 52, of which waited for: 29 -> 32; matrix products, arithmetic and copies ran while one was open for 13% -> 13% of each run, Pallas kernels for 0% -> 0%
where the time goes in v1:
time: 1760 us; the launch traced here: 1750 us
  waiting for transfers between devices  1190 us (68%)
  blocking collectives  216 us (12%)
  matrix products  140 us (8%)
  local copies, waits for them, and re-layouts  73.4 us (4%)
  other arithmetic  66.9 us (4%)
  starting transfers between devices  50.9 us (3%)
    reduce_scatter x1, waiting for transfers between devices, local(): lax.psum_scatter(grad_w_qkv, ('head', 'blk'), scatter_dimension=0, tiled=...  190 us
    reduce_scatter x1, waiting for transfers between devices, local(): lax.psum_scatter(grad_w_up, ('head', 'blk'), scatter_dimension=0, tiled=T...  187 us
    reduce_scatter x1, waiting for transfers between devices, local(): lax.psum_scatter(grad_w_down, ('head', 'blk'), scatter_dimension=0, tiled...  187 us
    all_gather x1, blocking collectives, local(): lax.all_gather(scale_attn, ('head', 'blk'), axis=0, tiled=True)  158 us
    reduce_scatter x1, waiting for transfers between devices, local(): lax.psum_scatter(grad_w_out, ('head', 'blk'), scatter_dimension=0, tiled=...  140 us
    reduce_scatter x1, waiting for transfers between devices, local(): lax.psum_scatter(grad_scale_attn, ('head', 'blk'), scatter_dimension=0, t...  134 us
    all_gather x1, waiting for transfers between devices, local(): lax.all_gather(w_down, ('head', 'blk'), axis=0, tiled=True)  74 us
    all_gather x1, waiting for transfers between devices, local(): lax.all_gather(w_up, ('head', 'blk'), axis=0, tiled=True)  71 us
  transfers between devices with their start and end apart: 52, of which 32 were waited for; matrix products, arithmetic and copies ran while one was open for 13% of the time, Pallas kernels for 0%

profile of v1, /device:TPU:14, one launch (start us, length us, event | category | flops | bytes accessed | tf_op | source)
XLA Modules:
  0.0 1748.4 jit_solution(11634983505463392191)
XLA Ops:
  10.6 10.6 collective-permute-done.5
  22.0 18.2 %collective-permute-done.6 = bf16[4,32,3072]{2,1,0:T(8,128)(2,1)S(1)} collective-permute-done((bf16[4,32,3072]{2,1,0:T(8,128)(2,1)S(1)}, bf16[4,32,3072]{2,1,0:T(8,128)(2,1)S(1)}, u32[]{:S(2)}, u32[]{:S(2)}) %collective-permute-start.6) | collective-permute-done | bytes 786464 | tf_op jit(solution)/shard_map/ppermute | solution.py:26
  41.3 34.2 %collective-permute-done.7 = bf16[8,32,3072]{2,1,0:T(8,128)(2,1)S(1)} collective-permute-done((bf16[8,32,3072]{2,1,0:T(8,128)(2,1)S(1)}, bf16[8,32,3072]{2,1,0:T(8,128)(2,1)S(1)}, u32[]{:S(2)}, u32[]{:S(2)}) %collective-permute-start.7) | collective-permute-done | bytes 1572896 | tf_op jit(solution)/shard_map/ppermute | solution.py:26
  76.7 2.7 collective-permute-start.8
  80.8 158.3 %all_gather.27 = bf16[256,1024]{1,0:T(8,128)(2,1)S(1)} all-gather(bf16[8,1024]{1,0:T(8,128)(2,1)} %param.23), channel_id=1, replica_groups=mesh['head'=4,'blk'=8] {'head','blk'}, dimensions={0}, use_global_device_ids=true | all-gather | bytes 540672 | tf_op jit(solution)/shard_map/all_gather | solution.py:151
  240.3 2.5 pad_maximum_fusion
  242.8 4.4 reverse_select_fusion
  247.2 8.7 copy.149
  256.0 4.5 fusion.49
  263.0 2.9 fusion.62
  267.3 21.9 %all_to_all.66 = bf16[4,2,49152]{2,1,0:T(2,128)(2,1)S(1)} all-to-all(bf16[4,2,49152]{2,1,0:T(2,128)(2,1)S(1)} %reshape.256), channel_id=1, replica_groups=mesh['head'=4,'blk'=8] {'head'}, dimensions={0} | all-to-all | bytes 1572864 | tf_op jit(solution)/shard_map/all_to_all | solution.py:179
  290.4 2.3 copy.183
  296.6 25.5 %all-gather.17.cloned.1.call-done = bf16[2,2048,1,256]{3,1,2,0:T(8,128)(2,1)} async-done(((bf16[2,256,1,256]{3,1,2,0:T(8,128)(2,1)}), bf16[2,2048,1,256]{3,1,2,0:T(8,128)(2,1)}) %all-gather.17.cloned.1.call-update) | async-done | bytes 2097168 | tf_op jit(solution)/shard_map/all_gather | solution.py:189
  322.2 30.4 %all-gather.19.cloned.1.call-done = bf16[2,2048,1,256]{3,1,2,0:T(8,128)(2,1)} async-done(((bf16[2,256,1,256]{3,1,2,0:T(8,128)(2,1)}), bf16[2,2048,1,256]{3,1,2,0:T(8,128)(2,1)}) %all-gather.19.cloned.1.call-update) | async-done | bytes 2097168 | tf_op jit(solution)/shard_map/all_gather | solution.py:190
  352.6 22.7 %while.37 = (s32[]{:T(128)}, f32[2,256,4]{1,2,0:T(4,128)S(1)}, f32[2,256,4]{1,2,0:T(4,128)S(1)}, f32[2,256,4,64]{1,3,2,0:T(8,128)S(1)}, bf16[2,2048,256]{2,1,0:T...) while((s32[]{:T(128)}, f32[2,256,4]{1,2,0:T(4,128)S(1)}, ...), condition=%wide.region_5.6_spmd.clone, body=%wide.region_2.5_spmd.clone.sunk | while | flops 138815488 | bytes 10354867 | solution.py:203
  376.2 5.1 all-to-all-start.1
  381.3 35.7 %all_gather.31 = bf16[256,1024]{1,0:T(8,128)(2,1)S(1)} all-gather(bf16[8,1024]{1,0:T(8,128)(2,1)S(1)} %copy-done.38), channel_id=1, replica_groups=mesh['head'=4,'blk'=8] {'head','blk'}, dimensions={0}, use_global_device_ids=true | all-gather | bytes 540672 | tf_op jit(solution)/shard_map/all_gather | solution.py:152
  421.3 71.0 %all-gather.11.cloned.1.call-done = bf16[1024,4096]{1,0:T(8,128)(2,1)} async-done(((bf16[32,4096]{1,0:T(8,128)(2,1)}), bf16[1024,4096]{1,0:T(8,128)(2,1)}) %all-gather.11.cloned.1.call-update) | async-done | bytes 8388624 | tf_op jit(solution)/shard_map/all_gather | solution.py:149
  492.3 4.7 fusion.65
  497.1 74.0 %all-gather.13.cloned.1.call-done = bf16[4096,1024]{1,0:T(8,128)(2,1)} async-done(((bf16[128,1024]{1,0:T(8,128)(2,1)}), bf16[4096,1024]{1,0:T(8,128)(2,1)}) %all-gather.13.cloned.1.call-update) | async-done | bytes 8388624 | tf_op jit(solution)/shard_map/all_gather | solution.py:150
  571.1 10.4 add_convert_fusion
  581.6 2.9 fusion.66
  586.7 2.5 convolution_convert_fusion
  590.7 3.9 all-to-all-start.2
  596.9 5.3 all-to-all-done.2
  605.0 171.6 %while.38 = (s32[]{:T(128)}, bf16[2,256,256]{1,2,0:T(8,128)(2,1)}, bf16[2,256,256]{1,2,0:T(8,128)(2,1)}, f32[2,256,256]{1,2,0:T(8,128)}, f32[2,256,256]{1,2,0:T(...) while((s32[]{:T(128)}, bf16[2,256,256]{1,2,0:T(8,128)(2,1)}, ...), condition=%wide.region_12.13_spmd.clone, body=%wide.region_11.12_spmd.clone.sunk | while | flops 341049344 | bytes 24928572 | solution.py:295
  629.3 2.4 collective-permute-start.1
  640.4 2.2 fusion.162
  646.0 2.8 collective-permute-done.3
  660.9 2.5 collective-permute-start.3
  683.8 2.2 fusion.162
  715.6 2.8 collective-permute-start.1
  768.7 2.2 fusion.162
  781.8 14.0 all-to-all-start.3
  797.9 12.9 all-to-all-done.3
  816.9 5.1 fusion.44
  824.7 2.7 fusion.68
  828.9 6.3 fusion.67
  836.5 8.2 fusion.69
  844.8 2.5 multiply_convert_fusion
  847.3 8.1 fusion.70
  856.5 5.4 fusion.34
  863.2 40.5 %reduce-scatter.17.cloned.1.call-done = f32[8,1024]{1,0:T(8,128)} async-done(((f32[256,1024]{1,0:T(8,128)}), f32[8,1024]{1,0:T(8,128)}) %reduce-scatter.17.cloned.1.call-update) | async-done | bytes 32784 | tf_op jit(solution)/shard_map/reduce_scatter | solution.py:341
  903.7 133.6 %reduce-scatter.15.cloned.1.call-done = f32[8,1024]{1,0:T(8,128)} async-done(((f32[256,1024]{1,0:T(8,128)}), f32[8,1024]{1,0:T(8,128)}) %reduce-scatter.15.cloned.1.call-update) | async-done | bytes 32784 | tf_op jit(solution)/shard_map/reduce_scatter | solution.py:340
  1037.3 139.5 %reduce-scatter.9.cloned.1.call-done = f32[32,1024]{1,0:T(8,128)} async-done(((f32[1024,1024]{1,0:T(8,128)}), f32[32,1024]{1,0:T(8,128)}) %reduce-scatter.9.cloned.1.call-update) | async-done | bytes 131088 | tf_op jit(solution)/shard_map/reduce_scatter | solution.py:337
  1176.8 189.8 %reduce-scatter.7.cloned.1.call-done = f32[32,3072]{1,0:T(8,128)} async-done(((f32[1024,3072]{1,0:T(8,128)}), f32[32,3072]{1,0:T(8,128)}) %reduce-scatter.7.cloned.1.call-update) | async-done | bytes 393232 | tf_op jit(solution)/shard_map/reduce_scatter | solution.py:336
  1366.6 187.4 %reduce-scatter.11.cloned.1.call-done = f32[32,4096]{1,0:T(8,128)} async-done(((f32[1024,4096]{1,0:T(8,128)}), f32[32,4096]{1,0:T(8,128)}) %reduce-scatter.11.cloned.1.call-update) | async-done | bytes 524304 | tf_op jit(solution)/shard_map/reduce_scatter | solution.py:338
  1554.0 187.3 %reduce-scatter.13.cloned.1.call-done = f32[128,1024]{1,0:T(8,128)} async-done(((f32[4096,1024]{1,0:T(8,128)}), f32[128,1024]{1,0:T(8,128)}) %reduce-scatter.13.cloned.1.call-update) | async-done | bytes 524304 | tf_op jit(solution)/shard_map/reduce_scatter | solution.py:339
  (441 shorter events, 228.8 us)
Async XLA Ops:
  7.2 315.0 %all-gather.17.cloned.1.call-start = ((), (), s32[]{:S(2)}) async-start(), calls=%async_computation.20 | async-start | bytes 2359296 | tf_op jit(solution)/shard_map/all_gather | solution.py:189
  10.0 11.2 collective-permute-start.5
  21.5 18.8 %collective-permute-start.6 = (bf16[4,32,3072]{2,1,0:T(8,128)(2,1)S(1)}, bf16[4,32,3072]{2,1,0:T(8,128)(2,1)S(1)}, u32[]{:S(2)}, u32[]{:S(2)}) collective-permute-start(bf16[4,32,3072]{2,1,0:T(8,128)(2,1)S(1)} %bitcast.278), channel_id=1, source_target_pairs={{0,4},{1,5},{2,6},{3,7},{4,0},{5,1},{6,2},{7,3},{8,12},{9,13},{10,... | collective-permute-start | bytes 2359304 | tf_op jit(solution)/shard_map/ppermute | solution.py:26
  40.8 34.8 %collective-permute-start.7 = (bf16[8,32,3072]{2,1,0:T(8,128)(2,1)S(1)}, bf16[8,32,3072]{2,1,0:T(8,128)(2,1)S(1)}, u32[]{:S(2)}, u32[]{:S(2)}) collective-permute-start(bf16[8,32,3072]{2,1,0:T(8,128)(2,1)S(1)} %bitcast.271), channel_id=1, source_target_pairs={{0,8},{1,9},{2,10},{3,11},{4,12},{5,13},{6,14},{7,15},{8,0},{9,1},... | collective-permute-start | bytes 4718600 | tf_op jit(solution)/shard_map/ppermute | solution.py:26
  76.7 163.6 %collective-permute-start.8 = (bf16[16,32,3072]{2,1,0:T(8,128)(2,1)S(1)}, bf16[16,32,3072]{2,1,0:T(8,128)(2,1)}, u32[]{:S(2)}, u32[]{:S(2)}) collective-permute-start(bf16[16,32,3072]{2,1,0:T(8,128)(2,1)S(1)} %bitcast.267), channel_id=1, source_target_pairs={{0,16},{1,17},{2,18},{3,19},{4,20},{5,21},{6,22},{7,23},{8,24},{9,... | collective-permute-start | bytes 9437192 | tf_op jit(solution)/shard_map/ppermute | solution.py:26
  293.8 58.7 %all-gather.19.cloned.1.call-start = ((), (), s32[]{:S(2)}) async-start(), calls=%async_computation.21 | async-start | bytes 2359296 | tf_op jit(solution)/shard_map/all_gather | solution.py:190
  294.6 122.9 %all-gather.9.cloned.1.call-start = ((), (), s32[]{:S(2)}) async-start(), calls=%async_computation.10 | async-start | bytes 2162688 | tf_op jit(solution)/shard_map/all_gather | solution.py:148
  295.3 197.0 %all-gather.11.cloned.1.call-start = ((), (), s32[]{:S(2)}) async-start(), calls=%async_computation.11 | async-start | bytes 8650752 | tf_op jit(solution)/shard_map/all_gather | solution.py:149
  295.9 275.2 %all-gather.13.cloned.1.call-start = ((), (), s32[]{:S(2)}) async-start(), calls=%async_computation.12 | async-start | bytes 8650752 | tf_op jit(solution)/shard_map/all_gather | solution.py:150
  376.2 41.2 %all-to-all-start.1 = ((bf16[2,256,256]{2,0,1:T(2,128)(2,1)}), bf16[2,256,256]{2,0,1:T(2,128)(2,1)S(1)}, u32[]{:S(2)}, u32[]{:S(2)}) async-start(bf16[2,256,256]{2,0,1:T(2,128)(2,1)} %copy.159), calls=%async_computation.1 | async-start | bytes 524288 | tf_op jit(solution)/shard_map/all_to_all | solution.py:207
  590.7 11.5 all-to-all-start.2
  594.5 222.3 %all-gather.15.cloned.1.call-start = ((), (), s32[]{:S(2)}) async-start(), calls=%async_computation.13 | async-start | bytes 6488064 | tf_op jit(solution)/shard_map/all_gather | solution.py:224
  606.7 19.1 %collective-permute-start = (bf16[2,256,256]{1,2,0:T(8,128)(2,1)}, bf16[2,256,256]{1,2,0:T(8,128)(2,1)}, u32[]{:S(2)}, u32[]{:S(2)}) collective-permute-start(bf16[2,256,256]{1,2,0:T(8,128)(2,1)} %copy.219), channel_id=1, source_target_pairs={{0,1},{1,2},{2,3},{3,4},{4,5},{5,6},{6,7},{7,0},{8,9},{9,10},{10,1... | collective-permute-start | bytes 786440 | tf_op jit(solution)/shard_map/while/body/eval_jaxpr/ppermute | solution.py:38
  608.4 17.5 collective-permute-start.1
  616.2 6.1 collective-permute-start.2
  617.8 7.3 collective-permute-start.3
  627.6 22.0 %collective-permute-start = (bf16[2,256,256]{1,2,0:T(8,128)(2,1)}, bf16[2,256,256]{1,2,0:T(8,128)(2,1)}, u32[]{:S(2)}, u32[]{:S(2)}) collective-permute-start(bf16[2,256,256]{1,2,0:T(8,128)(2,1)} %copy.219), channel_id=1, source_target_pairs={{0,1},{1,2},{2,3},{3,4},{4,5},{5,6},{6,7},{7,0},{8,9},{9,10},{10,1... | collective-permute-start | bytes 786440 | tf_op jit(solution)/shard_map/while/body/eval_jaxpr/ppermute | solution.py:38
  629.3 20.3 %collective-permute-start.1 = (bf16[2,256,256]{1,2,0:T(8,128)(2,1)}, bf16[2,256,256]{1,2,0:T(8,128)(2,1)}, u32[]{:S(2)}, u32[]{:S(2)}) collective-permute-start(bf16[2,256,256]{1,2,0:T(8,128)(2,1)} %copy.220), channel_id=1, source_target_pairs={{0,1},{1,2},{2,3},{3,4},{4,5},{5,6},{6,7},{7,0},{8,9},{9,10},{10,1... | collective-permute-start | bytes 786440 | tf_op jit(solution)/shard_map/while/body/eval_jaxpr/ppermute | solution.py:38
  638.1 6.1 collective-permute-start.2
  639.6 9.1 collective-permute-start.3
  651.3 18.9 %collective-permute-start = (bf16[2,256,256]{1,2,0:T(8,128)(2,1)}, bf16[2,256,256]{1,2,0:T(8,128)(2,1)}, u32[]{:S(2)}, u32[]{:S(2)}) collective-permute-start(bf16[2,256,256]{1,2,0:T(8,128)(2,1)} %copy.219), channel_id=1, source_target_pairs={{0,1},{1,2},{2,3},{3,4},{4,5},{5,6},{6,7},{7,0},{8,9},{9,10},{10,1... | collective-permute-start | bytes 786440 | tf_op jit(solution)/shard_map/while/body/eval_jaxpr/ppermute | solution.py:38
  653.0 17.2 collective-permute-start.1
  659.4 7.3 collective-permute-start.2
  660.9 8.5 collective-permute-start.3
  671.9 19.8 %collective-permute-start = (bf16[2,256,256]{1,2,0:T(8,128)(2,1)}, bf16[2,256,256]{1,2,0:T(8,128)(2,1)}, u32[]{:S(2)}, u32[]{:S(2)}) collective-permute-start(bf16[2,256,256]{1,2,0:T(8,128)(2,1)} %copy.219), channel_id=1, source_target_pairs={{0,1},{1,2},{2,3},{3,4},{4,5},{5,6},{6,7},{7,0},{8,9},{9,10},{10,1... | collective-permute-start | bytes 786440 | tf_op jit(solution)/shard_map/while/body/eval_jaxpr/ppermute | solution.py:38
  673.6 18.2 %collective-permute-start.1 = (bf16[2,256,256]{1,2,0:T(8,128)(2,1)}, bf16[2,256,256]{1,2,0:T(8,128)(2,1)}, u32[]{:S(2)}, u32[]{:S(2)}) collective-permute-start(bf16[2,256,256]{1,2,0:T(8,128)(2,1)} %copy.220), channel_id=1, source_target_pairs={{0,1},{1,2},{2,3},{3,4},{4,5},{5,6},{6,7},{7,0},{8,9},{9,10},{10,1... | collective-permute-start | bytes 786440 | tf_op jit(solution)/shard_map/while/body/eval_jaxpr/ppermute | solution.py:38
  682.1 6.1 collective-permute-start.2
  683.6 7.3 collective-permute-start.3
  693.5 18.8 %collective-permute-start = (bf16[2,256,256]{1,2,0:T(8,128)(2,1)}, bf16[2,256,256]{1,2,0:T(8,128)(2,1)}, u32[]{:S(2)}, u32[]{:S(2)}) collective-permute-start(bf16[2,256,256]{1,2,0:T(8,128)(2,1)} %copy.219), channel_id=1, source_target_pairs={{0,1},{1,2},{2,3},{3,4},{4,5},{5,6},{6,7},{7,0},{8,9},{9,10},{10,1... | collective-permute-start | bytes 786440 | tf_op jit(solution)/shard_map/while/body/eval_jaxpr/ppermute | solution.py:38
  695.1 17.1 collective-permute-start.1
  704.1 7.3 collective-permute-start.3
  713.9 20.5 %collective-permute-start = (bf16[2,256,256]{1,2,0:T(8,128)(2,1)}, bf16[2,256,256]{1,2,0:T(8,128)(2,1)}, u32[]{:S(2)}, u32[]{:S(2)}) collective-permute-start(bf16[2,256,256]{1,2,0:T(8,128)(2,1)} %copy.219), channel_id=1, source_target_pairs={{0,1},{1,2},{2,3},{3,4},{4,5},{5,6},{6,7},{7,0},{8,9},{9,10},{10,1... | collective-permute-start | bytes 786440 | tf_op jit(solution)/shard_map/while/body/eval_jaxpr/ppermute | solution.py:38
  715.6 18.8 %collective-permute-start.1 = (bf16[2,256,256]{1,2,0:T(8,128)(2,1)}, bf16[2,256,256]{1,2,0:T(8,128)(2,1)}, u32[]{:S(2)}, u32[]{:S(2)}) collective-permute-start(bf16[2,256,256]{1,2,0:T(8,128)(2,1)} %copy.220), channel_id=1, source_target_pairs={{0,1},{1,2},{2,3},{3,4},{4,5},{5,6},{6,7},{7,0},{8,9},{9,10},{10,1... | collective-permute-start | bytes 786440 | tf_op jit(solution)/shard_map/while/body/eval_jaxpr/ppermute | solution.py:38
  724.8 6.1 collective-permute-start.2
  726.3 7.3 collective-permute-start.3
  736.1 18.9 %collective-permute-start = (bf16[2,256,256]{1,2,0:T(8,128)(2,1)}, bf16[2,256,256]{1,2,0:T(8,128)(2,1)}, u32[]{:S(2)}, u32[]{:S(2)}) collective-permute-start(bf16[2,256,256]{1,2,0:T(8,128)(2,1)} %copy.219), channel_id=1, source_target_pairs={{0,1},{1,2},{2,3},{3,4},{4,5},{5,6},{6,7},{7,0},{8,9},{9,10},{10,1... | collective-permute-start | bytes 786440 | tf_op jit(solution)/shard_map/while/body/eval_jaxpr/ppermute | solution.py:38
  737.8 17.3 collective-permute-start.1
  746.9 7.3 collective-permute-start.3
  756.8 19.9 %collective-permute-start = (bf16[2,256,256]{1,2,0:T(8,128)(2,1)}, bf16[2,256,256]{1,2,0:T(8,128)(2,1)}, u32[]{:S(2)}, u32[]{:S(2)}) collective-permute-start(bf16[2,256,256]{1,2,0:T(8,128)(2,1)} %copy.219), channel_id=1, source_target_pairs={{0,1},{1,2},{2,3},{3,4},{4,5},{5,6},{6,7},{7,0},{8,9},{9,10},{10,1... | collective-permute-start | bytes 786440 | tf_op jit(solution)/shard_map/while/body/eval_jaxpr/ppermute | solution.py:38
  758.5 18.2 %collective-permute-start.1 = (bf16[2,256,256]{1,2,0:T(8,128)(2,1)}, bf16[2,256,256]{1,2,0:T(8,128)(2,1)}, u32[]{:S(2)}, u32[]{:S(2)}) collective-permute-start(bf16[2,256,256]{1,2,0:T(8,128)(2,1)} %copy.220), channel_id=1, source_target_pairs={{0,1},{1,2},{2,3},{3,4},{4,5},{5,6},{6,7},{7,0},{8,9},{9,10},{10,1... | collective-permute-start | bytes 786440 | tf_op jit(solution)/shard_map/while/body/eval_jaxpr/ppermute | solution.py:38
  768.5 7.3 collective-permute-start.3
  781.8 29.0 %all-to-all-start.3 = ((bf16[2,256,3,256]{3,0,2,1:T(2,128)(2,1)}), bf16[2,256,3,256]{3,0,2,1:T(2,128)(2,1)S(1)}, u32[]{:S(2)}, u32[]{:S(2)}) async-start(bf16[2,256,3,256]{3,0,2,1:T(2,128)(2,1)} %copy.169), calls=%async_computation.3 | async-start | bytes 1572864 | tf_op jit(solution)/shard_map/all_to_all | solution.py:307
  795.8 107.9 %reduce-scatter.17.cloned.1.call-start = ((), (), s32[]{:S(2)}) async-start(), calls=%async_computation.19 | async-start | bytes 1081344 | tf_op jit(solution)/shard_map/reduce_scatter | solution.py:341
  797.9 239.4 %reduce-scatter.15.cloned.1.call-start = ((), (), s32[]{:S(2)}) async-start(), calls=%async_computation.18 | async-start | bytes 1081344 | tf_op jit(solution)/shard_map/reduce_scatter | solution.py:340
  824.4 352.4 %reduce-scatter.9.cloned.1.call-start = ((), (), s32[]{:S(2)}) async-start(), calls=%async_computation.15 | async-start | bytes 4325376 | tf_op jit(solution)/shard_map/reduce_scatter | solution.py:337
  827.5 539.1 %reduce-scatter.7.cloned.1.call-start = ((), (), s32[]{:S(2)}) async-start(), calls=%async_computation.14 | async-start | bytes 12976128 | tf_op jit(solution)/shard_map/reduce_scatter | solution.py:336
  835.3 718.7 %reduce-scatter.11.cloned.1.call-start = ((), (), s32[]{:S(2)}) async-start(), calls=%async_computation.16 | async-start | bytes 17301504 | tf_op jit(solution)/shard_map/reduce_scatter | solution.py:338
  844.7 896.6 %reduce-scatter.13.cloned.1.call-start = ((), (), s32[]{:S(2)}) async-start(), calls=%async_computation.17 | async-start | bytes 17301504 | tf_op jit(solution)/shard_map/reduce_scatter | solution.py:339
  (56 other events, 2303.9 us)
Sparse Core Ops, SparseCore 0:
  293.9 28.1 all-gather.16
  324.6 27.8 all-gather.18
  355.4 56.8 all-gather.8
  415.1 77.2 all-gather.10
  495.1 76.0 all-gather.12
  597.9 73.0 all-gather.14
  799.4 104.2 reduce-scatter.16
  906.6 130.6 reduce-scatter.14
  1040.1 136.6 reduce-scatter.8
  1183.2 183.2 reduce-scatter.6
  1369.5 184.3 reduce-scatter.10
  1556.8 184.4 reduce-scatter.12
